TPU v7x, 128 devices: a whole 4x4x4 slice. The times are simulated.
128 devices in a mesh: req: 8 (over z, core), tok: 16 (over y, x).
Axes of the slice: x: 4, y: 4, z: 4, core: 2. Of those that a mesh axis runs over, the one named last changes fastest.
Arguments:
- draft_ids: int32 [32, 16], replicated, may hold values from 0 to 65535
- lengths: int32 [32], replicated, may hold values from 1 to 16384, as said below
- current_slot: int32 [32], replicated, may hold values from 0 to 31, as said below
- new_slot: int32 [32], replicated, may hold values from 0 to 31, as said below
- accepted: int32 [32], replicated, may hold values from 1 to 16, as said below
- embed_table: bfloat16 [65536, 3072], P(('req', 'tok')), may hold values from -6.5 to 6.5
- mixer_gain: float32 [3072], replicated, may hold values from 0.5 to 1.5
- query_weight: bfloat16 [3072, 768], replicated, may hold values from -0.3049512 to 0.3049512
- keyvalue_weight: bfloat16 [3072, 256], replicated, may hold values from -0.109375 to 0.109375
- key_cache: bfloat16 [32, 16384, 128], P('req', 'tok'), may hold values from -6 to 6
- value_cache: bfloat16 [32, 16384, 128], P('req', 'tok'), may hold values from -6 to 6
- attention_out: bfloat16 [768, 3072], P(None, 'tok'), may hold values from -0.21875 to 0.21875
- mamba_input: bfloat16 [3072, 2048], P(None, 'tok'), may hold values from -0.109375 to 0.109375
- mamba_gate: bfloat16 [3072, 2048], P(None, 'tok'), may hold values from -0.109375 to 0.109375
- state_proj: bfloat16 [3072, 512], replicated, may hold values from -0.02734375 to 0.02734375
- mamba_step: bfloat16 [3072, 16], P(None, 'tok'), may hold values from -0.109375 to 0.109375
- step_bias: float32 [16], P('tok'), may hold values from -4 to 0
- decay_log: float32 [16], P('tok'), may hold values from -2 to 1.5
- skip_gain: float32 [16], P('tok'), may hold values from 0.5 to 1.5
- states: float32 [32, 16, 128, 256], P('req', 'tok'), may hold values from -1.5 to 1.5
- mamba_out: bfloat16 [2048, 3072], P('tok'), may hold values from -0.125 to 0.125
- mlp_gain: float32 [3072], replicated, may hold values from 0.5 to 1.5
- gate_weight: bfloat16 [3072, 12288], P(None, ('req', 'tok')), may hold values from -0.109375 to 0.109375
- up_weight: bfloat16 [3072, 12288], P(None, ('req', 'tok')), may hold values from -0.109375 to 0.109375
- down_weight: bfloat16 [3072, 12288], P(None, ('req', 'tok')), may hold values from -0.0546875 to 0.0546875
Outputs:
- hidden_out: bfloat16 [512, 3072], P(('req', 'tok'))
- new_states: float32 [32, 16, 128, 256], P('req', 'tok')
Inputs may be any that keep to these rules, and one draw needn't show every extreme that they name: `lengths`: some request has exactly 16384 cached positions and some exactly one. `current_slot`: a permutation: each slot holds one request. `new_slot`: a permutation: each slot receives one request. `accepted`: some request accepts all 16 drafts and some exactly one.
All inputs are finite; a program needn't handle non-finite values.
Results may differ from a plain program's by a relative error of at most 0.02.
Values may be sent and summed in bfloat16 or wider, within the bound.
No kernel may reach another device: no remote copies, remote signals or barrier semaphores. Data moves between devices by JAX's collectives and lax.ppermute only.
A program may use at most 128 MiB of HBM per device.

v0:
```python
import jax
import jax.numpy as jnp
from jax import lax
from jax.sharding import PartitionSpec as P


def rms_rows(table_rows, norm_gain):
    values = table_rows.astype(jnp.float32)
    factor = lax.rsqrt(jnp.mean(values * values, axis=-1, keepdims=True) + 1e-05)
    return (values * factor * norm_gain).astype(jnp.bfloat16)


def inverse_of(mapping):
    places = jnp.arange(mapping.shape[0], dtype=jnp.int32)
    matches = mapping[None, :] == places[:, None]
    return jnp.sum(jnp.where(matches, places[None, :], 0), axis=1)


def recurrence(start_states, decay_rate, inputs, state_in, state_read, accept_count):

    def advance(state_pair, step_items):
        current, chosen = state_pair
        step_decay, step_input, step_in, step_read, step_index = step_items
        current = (
            step_decay[:, :, None, None] * current
            + step_input[..., None] * step_in[:, None, None, :]
        )
        readout = jnp.sum(current * step_read[:, None, None, :], axis=-1)
        chosen = jnp.where((accept_count == step_index + 1)[:, None, None, None], current, chosen)
        return ((current, chosen), readout)

    sequence = (
        jnp.swapaxes(decay_rate, 0, 1),
        jnp.swapaxes(inputs, 0, 1),
        jnp.swapaxes(state_in, 0, 1),
        jnp.swapaxes(state_read, 0, 1),
        jnp.arange(decay_rate.shape[1], dtype=jnp.int32),
    )
    (current, chosen), readouts = lax.scan(advance, (start_states, start_states), sequence)
    return (jnp.swapaxes(readouts, 0, 1), chosen)


def feed_units(block_rows, gate_cols, up_cols, down_cols):
    gate_part = jnp.dot(block_rows, gate_cols, preferred_element_type=jnp.float32)
    up_part = jnp.dot(block_rows, up_cols, preferred_element_type=jnp.float32)
    hidden = (jax.nn.silu(gate_part) * up_part).astype(jnp.bfloat16)
    return lax.dot_general(
        hidden, down_cols, (((1,), (1,)), ((), ())), preferred_element_type=jnp.float32
    )


def local(
    draft_ids,
    lengths,
    current_slot,
    new_slot,
    accepted,
    embed_table,
    mixer_gain,
    query_weight,
    keyvalue_weight,
    key_cache,
    value_cache,
    attention_out,
    mamba_input,
    mamba_gate,
    state_proj,
    mamba_step,
    step_bias,
    decay_log,
    skip_gain,
    states,
    mamba_out,
    mlp_gain,
    gate_weight,
    up_weight,
    down_weight,
):
    members = lax.axis_size("tok")
    group_index = lax.axis_index("req")
    member = lax.axis_index("tok")
    slots_dev, cache_dev, head_size = key_cache.shape
    draft_len = draft_ids.shape[1]
    group_tokens = slots_dev * draft_len
    vocab_dev = embed_table.shape[0]
    query_heads = query_weight.shape[1] // head_size
    heads_dev = step_bias.shape[0]
    mamba_head = mamba_input.shape[1] // heads_dev
    state_size = state_proj.shape[1] // 2
    slot_owner = inverse_of(current_slot)
    token_ids = jnp.take(draft_ids, slot_owner, axis=0).reshape(-1)
    vocab_start = (group_index * members + member) * vocab_dev
    wanted = token_ids - vocab_start
    inside = (wanted >= 0) & (wanted < vocab_dev)
    picked = jnp.take(embed_table, jnp.clip(wanted, 0, vocab_dev - 1), axis=0)
    embedded = lax.psum_scatter(
        jnp.where(inside[:, None], picked.astype(jnp.float32), 0.0),
        ("req", "tok"),
        scatter_dimension=0,
        tiled=True,
    ).astype(jnp.bfloat16)
    normed = rms_rows(embedded, mixer_gain)
    gathered = lax.all_gather(normed, "tok", axis=0, tiled=True)
    queries = jnp.dot(gathered, query_weight, preferred_element_type=jnp.float32).astype(
        jnp.bfloat16
    )
    queries = queries.reshape(slots_dev, draft_len, query_heads, head_size)
    keyvalue = jnp.dot(gathered, keyvalue_weight, preferred_element_type=jnp.float32).astype(
        jnp.bfloat16
    )
    keyvalue = keyvalue.reshape(slots_dev, draft_len, 2, head_size)
    local_owner = lax.dynamic_slice_in_dim(slot_owner, group_index * slots_dev, slots_dev)
    slot_length = jnp.take(lengths, local_owner)
    slot_accept = jnp.take(accepted, local_owner)
    score_scale = head_size ** (-0.5)
    positions = member * cache_dev + jnp.arange(cache_dev, dtype=jnp.int32)
    visible = (positions[None, :] < slot_length[:, None])[:, None, None, :]
    cache_scores = (
        jnp.einsum("sthd,spd->sthp", queries, key_cache, preferred_element_type=jnp.float32)
        * score_scale
    )
    local_max = jnp.max(jnp.where(visible, cache_scores, -1e30), axis=-1)
    cache_probs = jnp.where(visible, jnp.exp(cache_scores - local_max[..., None]), 0.0)
    local_total = jnp.sum(cache_probs, axis=-1)
    local_out = jnp.einsum(
        "sthp,spd->sthd",
        cache_probs.astype(jnp.bfloat16),
        value_cache,
        preferred_element_type=jnp.float32,
    )
    cache_max = lax.pmax(local_max, "tok")
    factor = jnp.exp(local_max - cache_max)
    cache_total, cache_out = (
        lax.psum((local_total * factor).astype(jnp.bfloat16), "tok").astype(jnp.float32),
        lax.psum((local_out * factor[..., None]).astype(jnp.bfloat16), "tok").astype(jnp.float32),
    )
    causal = (jnp.arange(draft_len)[None, :] <= jnp.arange(draft_len)[:, None])[None, :, None, :]
    draft_scores = (
        jnp.einsum("sthd,sud->sthu", queries, keyvalue[:, :, 0], preferred_element_type=jnp.float32)
        * score_scale
    )
    draft_max = jnp.max(jnp.where(causal, draft_scores, -1e30), axis=-1)
    joint_max = jnp.maximum(cache_max, draft_max)
    cache_factor = jnp.exp(cache_max - joint_max)
    draft_probs = jnp.where(causal, jnp.exp(draft_scores - joint_max[..., None]), 0.0)
    prob_total = cache_total * cache_factor + jnp.sum(draft_probs, axis=-1)
    summed = cache_out * cache_factor[..., None] + jnp.einsum(
        "sthu,sud->sthd",
        draft_probs.astype(jnp.bfloat16),
        keyvalue[:, :, 1],
        preferred_element_type=jnp.float32,
    )
    attended = (
        (summed / prob_total[..., None])
        .astype(jnp.bfloat16)
        .reshape(group_tokens, query_heads * head_size)
    )
    attn_proj = jnp.dot(attended, attention_out, preferred_element_type=jnp.float32)
    attn_rows = lax.all_to_all(
        attn_proj.astype(jnp.bfloat16), "tok", split_axis=0, concat_axis=1, tiled=True
    ).astype(attn_proj.dtype)
    mamba_x = jnp.dot(gathered, mamba_input, preferred_element_type=jnp.float32)
    mamba_x = mamba_x.reshape(slots_dev, draft_len, heads_dev, mamba_head)
    mamba_z = jnp.dot(gathered, mamba_gate, preferred_element_type=jnp.float32)
    mamba_z = mamba_z.reshape(slots_dev, draft_len, heads_dev, mamba_head)
    both_proj = jnp.dot(gathered, state_proj, preferred_element_type=jnp.float32)
    both_proj = both_proj.reshape(slots_dev, draft_len, 2, state_size)
    step_size = jax.nn.softplus(
        jnp.dot(gathered, mamba_step, preferred_element_type=jnp.float32) + step_bias
    ).reshape(slots_dev, draft_len, heads_dev)
    decay_rate = jnp.exp(-jnp.exp(decay_log) * step_size)
    readout, chosen = recurrence(
        states,
        decay_rate,
        step_size[..., None] * mamba_x,
        both_proj[:, :, 0],
        both_proj[:, :, 1],
        slot_accept,
    )
    readout = readout + skip_gain[None, None, :, None] * mamba_x
    gated = (
        (readout * jax.nn.silu(mamba_z))
        .astype(jnp.bfloat16)
        .reshape(group_tokens, heads_dev * mamba_head)
    )
    mamba_rows = lax.psum_scatter(
        jnp.dot(gated, mamba_out, preferred_element_type=jnp.float32).astype(jnp.bfloat16),
        "tok",
        scatter_dimension=0,
        tiled=True,
    ).astype(jnp.float32)
    mixed_rows = (embedded.astype(jnp.float32) + attn_rows + mamba_rows).astype(jnp.bfloat16)
    second = rms_rows(mixed_rows, mlp_gain)
    everything = lax.all_gather(second, ("req", "tok"), axis=0, tiled=True)
    mlp_rows = lax.psum_scatter(
        feed_units(everything, gate_weight, up_weight, down_weight),
        ("req", "tok"),
        scatter_dimension=0,
        tiled=True,
    )
    hidden_out = (mixed_rows.astype(jnp.float32) + mlp_rows).astype(jnp.bfloat16)
    every_state = lax.all_gather(chosen.astype(jnp.bfloat16), "req", axis=0, tiled=True).astype(
        chosen.dtype
    )
    incoming = inverse_of(new_slot)
    local_targets = lax.dynamic_slice_in_dim(incoming, group_index * slots_dev, slots_dev)
    sources = jnp.take(current_slot, local_targets)
    new_states = jnp.take(every_state, sources, axis=0)
    return (hidden_out, new_states)


def solution(mesh):
    return jax.shard_map(
        local,
        mesh=mesh,
        in_specs=(
            P(),
            P(),
            P(),
            P(),
            P(),
            P(("req", "tok"), None),
            P(),
            P(),
            P(),
            P("req", "tok", None),
            P("req", "tok", None),
            P(None, "tok"),
            P(None, "tok"),
            P(None, "tok"),
            P(),
            P(None, "tok"),
            P("tok"),
            P("tok"),
            P("tok"),
            P("req", "tok", None, None),
            P("tok", None),
            P(),
            P(None, ("req", "tok")),
            P(None, ("req", "tok")),
            P(None, ("req", "tok")),
        ),
        out_specs=(P(("req", "tok"), None), P("req", "tok", None, None)),
        check_vma=False,
    )
```

profile of v0, /device:TPU:1, one launch (start us, length us, event | category | flops | bytes accessed | tf_op | source)
XLA Modules:
  0.0 808.4 jit_solution(15467223869452533136)
XLA Ops:
  7.2 2.0 copy.142
  12.4 3.9 gather_fusion.1
  16.4 6.2 convert_select_fusion
  22.5 109.7 %all-reduce.11 = bf16[512,3072]{1,0:T(8,128)(2,1)} all-reduce(f32[512,3072]{1,0:T(8,128)} %convert_select_fusion), channel_id=2, replica_groups=mesh['req'=8,'tok'=16] {'req','tok'}, use_global_device_ids=true, to_apply=%region_1.2.clone | all-reduce | flops 1572864 | bytes 9437184
  133.7 19.8 %all-gather = bf16[16,4,3072]{2,1,0:T(4,128)(2,1)} all-gather(bf16[1,4,3072]{2,1,0:T(4,128)(2,1)S(1)} %fusion.44), channel_id=1, replica_groups=mesh['req'=8,'tok'=16] {'tok'}, dimensions={0}, use_global_device_ids=true | all-gather | bytes 417792 | tf_op jit(solution)/shard_map/all_gather | solution.py:103
  154.7 3.9 convolution_convert_fusion.1
  166.3 2.9 select_reduce_fusion
  169.2 57.9 %pmax.7 = f32[4,16,6]{1,2,0:T(8,128)} all-reduce(f32[4,16,6]{1,2,0:T(8,128)S(1)} %get-tuple-element.145), channel_id=1, replica_groups=mesh['req'=8,'tok'=16] {'tok'}, use_global_device_ids=true, to_apply=%region_4.6 | all-reduce | flops 384 | bytes 3072 | tf_op jit(solution)/shard_map/pmax | solution.py:131
  227.1 2.4 fusion.1
  229.5 2.4 convolution_convert_fusion.2
  234.8 3.2 fusion.54
  241.3 2.0 fusion.53
  255.5 165.3 %while.14 = (s32[]{:T(128)}, f32[4,1,128,256]{3,2,1,0:T(8,128)}, bf16[4,1,128,256]{3,2,1,0:T(8,128)(2,1)}, f32[16,4,1,128]{3,0,1,2:T(8,128)}, f32[16,4,1]{1,2,0:...) while((s32[]{:T(128)}, f32[4,1,128,256]{3,2,1,0:T(8,128)}, ...), condition=%wide.region_12.14_spmd, body=%wide.region_10.13_spmd.sunk | while | flops 785927 | bytes 2134257 | solution.py:39
  257.6 2.6 multiply_reduce_fusion.2
  268.0 2.6 multiply_reduce_fusion.2
  273.0 1.9 broadcast_select_fusion.4
  278.3 2.6 multiply_reduce_fusion.2
  283.3 1.9 broadcast_select_fusion.4
  288.7 2.6 multiply_reduce_fusion.2
  293.7 1.9 broadcast_select_fusion.4
  299.1 2.6 multiply_reduce_fusion.2
  309.4 2.6 multiply_reduce_fusion.2
  319.6 2.6 multiply_reduce_fusion.2
  330.0 2.6 multiply_reduce_fusion.2
  340.3 2.6 multiply_reduce_fusion.2
  350.6 2.6 multiply_reduce_fusion.2
  361.0 2.6 multiply_reduce_fusion.2
  371.3 2.6 multiply_reduce_fusion.2
  381.6 2.6 multiply_reduce_fusion.2
  391.9 2.6 multiply_reduce_fusion.2
  402.3 2.6 multiply_reduce_fusion.2
  412.6 2.6 multiply_reduce_fusion.2
  422.9 2.0 select_reduce_fusion.1
  425.7 2.2 convolution_convert_fusion
  428.6 2.8 fusion.5
  431.4 29.1 %psum.15 = bf16[4,16,6]{1,2,0:T(8,128)(2,1)S(1)} all-reduce(bf16[4,16,6]{1,2,0:T(8,128)(2,1)S(1)} %get-tuple-element.132), channel_id=1, replica_groups=mesh['req'=8,'tok'=16] {'tok'}, use_global_device_ids=true, to_apply=%region_8.10 | all-reduce | flops 384 | bytes 1536 | tf_op jit(solution)/shard_map/psum | solution.py:134
  462.2 68.0 %all-reduce.10.cloned.1.call-done = (bf16[4,16,6,128]{3,1,2,0:T(8,128)(2,1)}, bf16[64,3072]{1,0:T(8,128)(2,1)}) async-done(((bf16[4,16,6,128]{3,1,2,0:T(8,128)(2,1)}, bf16[64,3072]{1,0:T(8,128)(2,1)}), (bf16[4,16,6,128]{3,1,2,0:T(8,128)(2,1)}, bf16[64,3072]{1,0:T(8,128)(2,1)})) %all-reduce.10.cloned.1.call-update) | async-done | bytes 491536 | tf_op jit(solution)/shard_map/psum | solution.py:135
  532.4 3.8 all-to-all-start
  538.2 4.4 all-to-all-done
  546.1 66.2 %all-gather.7.cloned.1.call-done = bf16[128,4,3072]{2,1,0:T(4,128)(2,1)} async-done(((bf16[1,4,3072]{2,1,0:T(4,128)(2,1)}), bf16[128,4,3072]{2,1,0:T(4,128)(2,1)}) %all-gather.7.cloned.1.call-update) | async-done | bytes 3145744 | tf_op jit(solution)/shard_map/all_gather | solution.py:194
  612.3 6.0 reshape.403
  618.3 3.2 fusion.56
  621.4 6.9 fusion.7
  629.7 7.2 all-gather.5.cloned.1.call-done
  636.9 4.1 bitcast_convert_fusion
  641.0 3.6 gather_fusion.2
  644.6 1.9 fusion.15
  646.5 153.9 %all-reduce.8.cloned.1.call-done = f32[512,3072]{1,0:T(8,128)} async-done(((f32[512,3072]{1,0:T(8,128)}), f32[512,3072]{1,0:T(8,128)}) %all-reduce.8.cloned.1.call-update) | async-done | bytes 6291472
  (205 shorter events, 153.6 us)
Async XLA Ops:
  7.2 5.3 copy-start
  7.2 523.0 %all-reduce.10.cloned.1.call-start = ((), (), s32[]{:S(2)}) async-start(), calls=%async_computation.4 | async-start | bytes 983040 | tf_op jit(solution)/shard_map/psum | solution.py:135
  22.5 110.6 %copy-start.10 = (f32[3072]{0:T(1024)S(1)}, f32[3072]{0:T(1024)}, u32[]{:S(2)}) copy-start(f32[3072]{0:T(1024)} %param.35) | copy-start | bytes 36868
  133.1 0.6 copy-start.5
  153.5 6.7 copy-start.12
  153.6 8.6 %copy-start.1 = (s32[32]{0:T(128)S(1)}, s32[32]{0:T(128)}, u32[]{:S(2)}) copy-start(s32[32]{0:T(128)} %param.30) | copy-start | bytes 388
  154.7 8.6 %copy-start.2 = (s32[32]{0:T(128)S(1)}, s32[32]{0:T(128)}, u32[]{:S(2)}) copy-start(s32[32]{0:T(128)} %param.33) | copy-start | bytes 388
  165.7 0.6 copy-start.8
  422.2 39.3 %copy-start.7 = (f32[4,16,6]{1,2,0:T(8,128)S(1)}, f32[4,16,6]{1,2,0:T(8,128)}, u32[]{:S(2)}) copy-start(f32[4,16,6]{1,2,0:T(8,128)} %pmax.7) | copy-start | bytes 4612
  422.2 108.0 %copy-start.9 = (bf16[4,16,1,128]{3,2,1,0:T(2,128)(2,1)S(1)}, bf16[4,16,1,128]{3,2,1,0:T(2,128)(2,1)}, u32[]{:S(2)}) copy-start(bf16[4,16,1,128]{3,2,1,0:T(2,128)(2,1)} %get-tuple-element.140) | copy-start | bytes 49156
  425.7 105.8 %copy-start.4 = (bf16[768,192]{0,1:T(8,128)(2,1)S(1)}, bf16[768,192]{0,1:T(8,128)(2,1)}, u32[]{:S(2)}) copy-start(bf16[768,192]{0,1:T(8,128)(2,1)} %param.40) | copy-start | bytes 884740
  427.9 114.9 %copy-start.6 = (bf16[4,3072]{1,0:T(4,128)(2,1)S(1)}, bf16[4,3072]{1,0:T(4,128)(2,1)}, u32[]{:S(2)}) copy-start(bf16[4,3072]{1,0:T(4,128)(2,1)} %copy-done.5) | copy-start | bytes 73732
  532.4 10.3 %all-to-all-start = ((bf16[16,4,192]{2,1,0:T(4,128)(2,1)}), bf16[16,4,192]{2,1,0:T(4,128)(2,1)S(1)}, u32[]{:S(2)}, u32[]{:S(2)}) async-start(bf16[16,4,192]{2,1,0:T(4,128)(2,1)} %all_to_all.10), calls=%async_computation | async-start | bytes 65536 | tf_op jit(solution)/shard_map/all_to_all | solution.py:159
  536.2 76.1 %all-gather.7.cloned.1.call-start = ((), (), s32[]{:S(2)}) async-start(), calls=%async_computation.2 | async-start | bytes 3170304 | tf_op jit(solution)/shard_map/all_gather | solution.py:194
  545.2 91.8 %all-gather.5.cloned.1.call-start = ((), (), s32[]{:S(2)}) async-start(), calls=%async_computation.1 | async-start | bytes 2359296 | tf_op jit(solution)/shard_map/all_gather | solution.py:202
  545.9 254.5 %all-reduce.8.cloned.1.call-start = ((), (), s32[]{:S(2)}) async-start(), calls=%async_computation.3 | async-start | bytes 12582912
  628.3 0.7 copy-start.11
  628.3 0.7 copy-start.3
Sparse Core Ops, SparseCore 0:
  431.5 98.6 all-reduce.9
  545.3 66.9 all-gather.6
  614.1 22.7 all-gather.4
  642.4 157.9 all-reduce.7
where the time goes:
time: 814 us; the launch traced here: 808 us
  waiting for transfers between devices  300 us (37%)
  blocking collectives  216 us (27%)
  other arithmetic  113 us (14%)
  local copies, waits for them, and re-layouts  112 us (14%)
  matrix products  35.8 us (4%)
  between operations  16.7 us (2%)
  loops' own time  9.92 us (1%)
    unnamed x5, waiting for transfers between devices  155 us
    unnamed x1, blocking collectives  110 us
    psum x1, waiting for transfers between devices, local(): lax.psum((local_out * factor[..., None]).astype(jnp.bfloat16), 'tok')  68 us
    all_gather x1, waiting for transfers between devices, local(): everything = lax.all_gather(second, ('req', 'tok'), axis=0, tiled=True)  66.2 us
    pmax x1, blocking collectives, local(): cache_max = lax.pmax(local_max, 'tok')  57.9 us
    reduce_sum x16, other arithmetic, advance(): readout = jnp.sum(current * step_read[:, None, None, :], axis=-1)  41 us
    select_n x16, other arithmetic, advance(): jnp.where((accept_count == step_index + 1)[:, None, None, None], current,...  31 us
    dynamic_slice x32, local copies, waits for them, and re-layouts, recurrence(): lax.scan(advance, (start_states, start_states), sequence)  30.9 us
  transfers between devices with their start and end apart: 5, of which 5 were waited for; matrix products, arithmetic and copies ran while one was open for 4% of the time, Pallas kernels for 0%

commit v1 on v0

--- a/solution.py
+++ b/solution.py
@@ -100,7 +100,9 @@
         tiled=True,
     ).astype(jnp.bfloat16)
     normed = rms_rows(embedded, mixer_gain)
-    gathered = lax.all_gather(normed, "tok", axis=0, tiled=True)
+    gathered = jnp.concatenate(
+        lax.all_to_all(jnp.stack([normed] * lax.axis_size("tok")), "tok", 0, 0), axis=0
+    )
     queries = jnp.dot(gathered, query_weight, preferred_element_type=jnp.float32).astype(
         jnp.bfloat16
     )

time: 814 us -> 629 us (0.77)
  other arithmetic: 113 us -> 25.6 us
  local copies, waits for them, and re-layouts: 112 us -> 37.2 us
  blocking collectives: 216 us -> 199 us
  matrix products: 35.8 us -> 27.4 us
    reduce_sum x16, other arithmetic: 41 us -> 5.23 us  [advance(): readout = jnp.sum(current * step_read[:, None, None, :], axis=-1)]
    select_n x16, other arithmetic: 31 us -> 2 us  [advance(): jnp.where((accept_count == step_index + 1)[:, None, None, None], current,...]
    dynamic_slice x32 -> x80, local copies, waits for them, and re-layouts: 30.9 us -> 9.99 us  [recurrence(): lax.scan(advance, (start_states, start_states), sequence)]
    dynamic_update_slice x16, local copies, waits for them, and re-layouts: 21.3 us -> 0.6 us  [recurrence(): lax.scan(advance, (start_states, start_states), sequence)]
    all_gather x1 -> x0, blocking collectives: 19.8 us -> none  [local(): gathered = lax.all_gather(normed, 'tok', axis=0, tiled=True)]
    mul x16 -> x0, local copies, waits for them, and re-layouts: 11 us -> none  [advance(): readout = jnp.sum(current * step_read[:, None, None, :], axis=-1)]
    mul x16, local copies, waits for them, and re-layouts: 10.3 us -> 0.15 us  [advance(): step_decay[:, :, None, None] * current]
    eq x16, other arithmetic: 10 us -> 0.1 us  [advance(): accept_count == step_index + 1]
  transfers between devices with their start and end apart: 5 -> 6, of which waited for: 5 -> 6; matrix products, arithmetic and copies ran while one was open for 4% -> 5% of each run, Pallas kernels for 0% -> 0%
where the time goes in v1:
time: 629 us; the launch traced here: 627 us
  waiting for transfers between devices  301 us (48%)
  blocking collectives  199 us (32%)
  local copies, waits for them, and re-layouts  37.2 us (6%)
  matrix products  27.4 us (4%)
  other arithmetic  25.6 us (4%)
  between operations  16.8 us (3%)
  loops' own time  11.5 us (2%)
  starting transfers between devices  9.23 us (1%)
    unnamed x5, waiting for transfers between devices  155 us
    unnamed x1, blocking collectives  110 us
    all_gather x1, waiting for transfers between devices, local(): everything = lax.all_gather(second, ('req', 'tok'), axis=0, tiled=True)  66.3 us
    psum x1, waiting for transfers between devices, local(): lax.psum((local_out * factor[..., None]).astype(jnp.bfloat16), 'tok')  63.4 us
    pmax x1, blocking collectives, local(): cache_max = lax.pmax(local_max, 'tok')  59.9 us
    psum x1, blocking collectives, local(): lax.psum((local_total * factor).astype(jnp.bfloat16), 'tok')  29.1 us
  transfers between devices with their start and end apart: 6, of which 6 were waited for; matrix products, arithmetic and copies ran while one was open for 5% of the time, Pallas kernels for 0%

profile of v1, /device:TPU:1, one launch (start us, length us, event | category | flops | bytes accessed | tf_op | source)
XLA Modules:
  0.0 627.3 jit_solution(11211211360543480838)
XLA Ops:
  7.2 2.0 copy.154
  9.2 0.8 select_reduce_fusion.3
  10.0 0.8 copy.72
  11.8 3.9 gather_fusion.1
  15.7 6.2 convert_select_fusion
  21.9 109.7 %all-reduce.11 = bf16[512,3072]{1,0:T(8,128)(2,1)} all-reduce(f32[512,3072]{1,0:T(8,128)} %convert_select_fusion), channel_id=2, replica_groups=mesh['req'=8,'tok'=16] {'req','tok'}, use_global_device_ids=true, to_apply=%region_1.2.clone | all-reduce | flops 1572864 | bytes 9437184
  131.6 0.9 fusion.34
  132.7 0.9 stack.2
  133.5 5.1 all-to-all-start
  138.9 0.6 gather_fusion.3
  139.5 0.6 gather_fusion.4
  141.5 4.7 copy.93
  147.0 0.7 all-to-all-done
  147.8 3.3 convolution_convert_fusion.1
  151.2 1.8 select_reduce_fusion
  153.0 59.9 %pmax.7 = f32[4,16,6]{1,2,0:T(8,128)S(1)} all-reduce(f32[4,16,6]{1,2,0:T(8,128)S(1)} %get-tuple-element.145), channel_id=1, replica_groups=mesh['req'=8,'tok'=16] {'tok'}, use_global_device_ids=true, to_apply=%region_4.6 | all-reduce | flops 384 | bytes 3072 | tf_op jit(solution)/shard_map/pmax | solution.py:133
  213.3 1.8 convolution_convert_fusion.2
  215.2 1.4 fusion.53
  217.1 0.9 reshape.420
  218.0 3.1 fusion.16
  221.2 29.6 %while.14 = (s32[]{:T(128)}, f32[4,1,128,256]{3,2,1,0:T(8,128)S(1)}, bf16[4,1,128,256]{3,2,1,0:T(8,128)(2,1)S(1)}, f32[16,4,1,128]{3,0,1,2:T(8,128)S(1)}, f32[16...) while((s32[]{:T(128)}, ...), condition=%wide.region_12.14_spmd, body=%wide.region_10.13_spmd.sunk | while | flops 785927 | bytes 2150641 | solution.py:39
  229.0 0.6 dynamic_slice.42
  234.5 0.6 dynamic_slice.42
  240.1 0.6 dynamic_slice.42
  250.7 1.5 fusion.54
  252.6 2.2 convolution_convert_fusion
  254.9 2.3 fusion.5
  257.2 29.1 %psum.15 = bf16[4,16,6]{1,2,0:T(8,128)(2,1)S(1)} all-reduce(bf16[4,16,6]{1,2,0:T(8,128)(2,1)S(1)} %get-tuple-element.132), channel_id=1, replica_groups=mesh['req'=8,'tok'=16] {'tok'}, use_global_device_ids=true, to_apply=%region_8.10 | all-reduce | flops 384 | bytes 1536 | tf_op jit(solution)/shard_map/psum | solution.py:136
  286.4 63.4 %all-reduce.10.cloned.1.call-done = (bf16[4,16,6,128]{3,1,2,0:T(8,128)(2,1)}, bf16[64,3072]{1,0:T(8,128)(2,1)}) async-done(((bf16[4,16,6,128]{3,1,2,0:T(8,128)(2,1)}, bf16[64,3072]{1,0:T(8,128)(2,1)}), (bf16[4,16,6,128]{3,1,2,0:T(8,128)(2,1)}, bf16[64,3072]{1,0:T(8,128)(2,1)})) %all-reduce.10.cloned.1.call-update) | async-done | bytes 491536 | tf_op jit(solution)/shard_map/psum | solution.py:137
  349.8 1.1 fusion.4
  351.2 0.6 all_to_all.14
  351.9 3.8 all-to-all-start.1
  357.2 5.0 all-to-all-done.1
  362.3 1.0 fusion.39
  363.3 0.7 fusion.45
  364.0 0.7 all-gather.4.cloned.1.call-update
  364.8 66.3 %all-gather.6.cloned.1.call-done = bf16[128,4,3072]{2,1,0:T(4,128)(2,1)} async-done(((bf16[1,4,3072]{2,1,0:T(4,128)(2,1)}), bf16[128,4,3072]{2,1,0:T(4,128)(2,1)}) %all-gather.6.cloned.1.call-update) | async-done | bytes 3145744 | tf_op jit(solution)/shard_map/all_gather | solution.py:196
  431.1 4.5 reshape.407
  435.6 2.2 fusion.55
  437.8 6.0 fusion.7
  443.8 0.6 copy-done.4
  444.4 0.6 gather_fusion.5
  445.1 10.7 %all-gather.4.cloned.1.call-done = bf16[32,1,128,256]{3,2,1,0:T(8,128)(2,1)} async-done(((bf16[4,1,128,256]{3,2,1,0:T(8,128)(2,1)}), bf16[32,1,128,256]{3,2,1,0:T(8,128)(2,1)}) %all-gather.4.cloned.1.call-update) | async-done | bytes 2097168 | tf_op jit(solution)/shard_map/all_gather | solution.py:204
  455.8 4.0 bitcast_convert_fusion
  459.9 3.6 gather_fusion.2
  463.4 1.9 fusion.15
  465.4 153.9 %all-reduce.8.cloned.1.call-done = f32[512,3072]{1,0:T(8,128)} async-done(((f32[512,3072]{1,0:T(8,128)}), f32[512,3072]{1,0:T(8,128)}) %all-reduce.8.cloned.1.call-update) | async-done | bytes 6291472
  619.3 1.5 fusion.42
  (239 shorter events, 20.9 us)
Async XLA Ops:
  7.2 4.6 copy-start
  21.9 110.7 %copy-start.8 = (f32[3072]{0:T(1024)S(1)}, f32[3072]{0:T(1024)}, u32[]{:S(2)}) copy-start(f32[3072]{0:T(1024)} %param.35) | copy-start | bytes 36868
  21.9 116.8 %copy-start.11 = (s32[32]{0:T(128)S(1)}, s32[32]{0:T(128)}, u32[]{:S(2)}) copy-start(s32[32]{0:T(128)} %param.32) | copy-start | bytes 388
  21.9 117.0 %copy-start.2 = (s32[32]{0:T(128)S(1)}, s32[32]{0:T(128)}, u32[]{:S(2)}) copy-start(s32[32]{0:T(128)} %param.30) | copy-start | bytes 388
  21.9 117.6 %copy-start.3 = (s32[32]{0:T(128)S(1)}, s32[32]{0:T(128)}, u32[]{:S(2)}) copy-start(s32[32]{0:T(128)} %param.33) | copy-start | bytes 388
  133.5 14.2 %all-to-all-start = ((bf16[16,4,3072]{2,1,0:T(4,128)(2,1)}), bf16[16,4,3072]{2,1,0:T(4,128)(2,1)S(1)}, u32[]{:S(2)}, u32[]{:S(2)}) async-start(bf16[16,4,3072]{2,1,0:T(4,128)(2,1)} %stack.2), calls=%async_computation | async-start | bytes 786432 | tf_op jit(solution)/shard_map/all_to_all | solution.py:104
  138.6 211.2 %all-reduce.10.cloned.1.call-start = ((), (), s32[]{:S(2)}) async-start(), calls=%async_computation.5 | async-start | bytes 983040 | tf_op jit(solution)/shard_map/psum | solution.py:137
  141.5 4.7 copy-start.5
  153.0 63.6 %copy-start.10 = (bf16[3072,1]{0,1:T(2,128)(2,1)S(1)}, bf16[3072,1]{0,1:T(2,128)(2,1)}, u32[]{:S(2)}) copy-start(bf16[3072,1]{0,1:T(2,128)(2,1)} %param.44) | copy-start | bytes 18436
  250.7 6.5 %copy-start.6 = (bf16[4,1,128,256]{3,2,1,0:T(8,128)(2,1)}, bf16[4,1,128,256]{3,2,1,0:T(8,128)(2,1)S(1)}, u32[]{:S(2)}) copy-start(bf16[4,1,128,256]{3,2,1,0:T(8,128)(2,1)S(1)} %get-tuple-element.57) | copy-start | bytes 786436
  252.6 98.4 %copy-start.7 = (bf16[768,192]{0,1:T(8,128)(2,1)S(1)}, bf16[768,192]{0,1:T(8,128)(2,1)}, u32[]{:S(2)}) copy-start(bf16[768,192]{0,1:T(8,128)(2,1)} %param.40) | copy-start | bytes 884740
  254.8 101.1 %copy-start.12 = (u32[128]{0:T(128)S(1)}, u32[128]{0:T(128)}, u32[]{:S(2)}) copy-start(u32[128]{0:T(128)} %constant.131) | copy-start | bytes 1540
  254.9 108.4 %copy-start.9 = (f32[3072]{0:T(1024)S(1)}, f32[3072]{0:T(1024)}, u32[]{:S(2)}) copy-start(f32[3072]{0:T(1024)} %param.50) | copy-start | bytes 36868
  351.9 10.3 %all-to-all-start.1 = ((bf16[16,4,192]{2,1,0:T(4,128)(2,1)}), bf16[16,4,192]{2,1,0:T(4,128)(2,1)S(1)}, u32[]{:S(2)}, u32[]{:S(2)}) async-start(bf16[16,4,192]{2,1,0:T(4,128)(2,1)} %all_to_all.14), calls=%async_computation.1 | async-start | bytes 65536 | tf_op jit(solution)/shard_map/all_to_all | solution.py:161
  355.7 75.4 %all-gather.6.cloned.1.call-start = ((), (), s32[]{:S(2)}) async-start(), calls=%async_computation.3 | async-start | bytes 3170304 | tf_op jit(solution)/shard_map/all_gather | solution.py:196
  364.0 91.9 %all-gather.4.cloned.1.call-start = ((), (), s32[]{:S(2)}) async-start(), calls=%async_computation.2 | async-start | bytes 2359296 | tf_op jit(solution)/shard_map/all_gather | solution.py:204
  364.7 254.6 %all-reduce.8.cloned.1.call-start = ((), (), s32[]{:S(2)}) async-start(), calls=%async_computation.4 | async-start | bytes 12582912
  443.8 0.7 copy-start.4
  445.1 175.7 %copy-start.1 = (bf16[512,3072]{1,0:T(8,128)(2,1)S(1)}, bf16[512,3072]{1,0:T(8,128)(2,1)}, u32[]{:S(2)}) copy-start(bf16[512,3072]{1,0:T(8,128)(2,1)} %param.34) | copy-start | bytes 9437188
Sparse Core Ops, SparseCore 0:
  257.3 92.4 all-reduce.9
  364.1 66.9 all-gather.5
  432.9 22.8 all-gather.3
  461.3 157.9 all-reduce.7
